TPU v7x, 32 devices: a whole 2x2x4 slice. The times are simulated.
32 devices in a mesh: row: 8 (over z, y), col: 4 (over x, core).
Axes of the slice: x: 2, y: 2, z: 4, core: 2. Of those that a mesh axis runs over, the one named last changes fastest.
Arguments:
- ancestor: float32 [1024, 1024], P('row', 'col'), may hold values from -0.1875 to 0.1875
- factor: float32 [1024, 16, 128], P(('row', 'col')), may hold values from -1.5 to 1.5
- diag_inv: float32 [16, 128, 128], replicated, may hold values from -6 to 6
- structure: int32 [16, 96], replicated, may hold values from 0 to 127, as said below
Outputs:
- inverse_panel: float32 [1024, 16, 128], P(('row', 'col'))
- inverse_diagonal: float32 [16, 128, 128], replicated
Inputs may be any that keep to these rules, and one draw needn't show every extreme that they name: Each row of structure lists 96 different block numbers, in no particular order.
All inputs are finite; a program needn't handle non-finite values.
Results may differ from a plain program's by a relative error of at most 0.00007.
Values sent between devices are 32-bit elements; how exact they have to be, the bound alone decides.
A program may use at most 64 MiB of HBM per device.

v0:
```python
import jax
import jax.numpy as jnp
from jax import lax
from jax.sharding import PartitionSpec as P

RB = 8


def per_device(ancestor, factor, diag_inv, structure):
    row_devices = lax.axis_size("row")
    col_devices = lax.axis_size("col")
    ratio = row_devices // col_devices
    local_rows = factor.shape[0]
    width = factor.shape[2]
    first_row = (lax.axis_index("row") * col_devices + lax.axis_index("col")) * local_rows
    block_ids = (first_row + jnp.arange(local_rows, dtype=jnp.int32)) // RB
    matches = block_ids[:, None, None] == structure[None, :, :]
    row_mask = jnp.any(matches, axis=2).astype(jnp.float32)
    masked = factor * row_mask[:, :, None]
    count_sib = masked.shape[1]
    spread = masked.reshape(local_rows, count_sib * width)
    strided = lax.all_gather(spread, "row", axis=0, tiled=True)
    grouped = strided.reshape(col_devices, ratio, local_rows, count_sib * width)
    swapped = lax.all_to_all(grouped, "col", split_axis=0, concat_axis=0, tiled=True)
    columns = jnp.transpose(swapped, (1, 0, 2, 3)).reshape(
        ratio * col_devices * local_rows, count_sib * width
    )
    summed = lax.psum_scatter(
        jnp.dot(
            ancestor, columns, precision=lax.Precision.HIGHEST, preferred_element_type=jnp.float32
        ),
        "col",
        scatter_dimension=0,
        tiled=True,
    )
    panel = -summed.reshape(local_rows, count_sib, width)
    panel = panel * row_mask[:, :, None]
    local_update = jnp.einsum("bsw,bsv->swv", masked, panel, precision=lax.Precision.HIGHEST)
    total_update = lax.psum(local_update, ("row", "col"))
    return (panel, diag_inv - total_update)


def solution(mesh):
    placed = (P("row", "col"), P(("row", "col"), None, None), P(), P())
    return jax.shard_map(
        per_device,
        mesh=mesh,
        in_specs=placed,
        out_specs=(P(("row", "col"), None, None), P()),
        check_vma=False,
    )
```

profile of v0, /device:TPU:0, one launch (start us, length us, event | category | flops | bytes accessed | tf_op | source)
XLA Modules:
  0.0 264.8 jit_solution(8581905215952985030)
XLA Ops:
  7.2 0.0 copy-start
  7.2 0.0 all-gather.2.cloned.1.call-start
  7.2 1.4 compare_reduce_fusion
  8.7 1.1 broadcast_multiply_fusion.1
  9.7 0.8 copy.32
  10.5 0.0 all-gather.2.cloned.1.call-update
  10.6 0.0 reduce-scatter.4.cloned.1.call-start
  10.6 51.9 %all-gather.2.cloned.1.call-done = f32[256,2048]{1,0:T(8,128)} async-done(((f32[32,2048]{1,0:T(8,128)}), f32[256,2048]{1,0:T(8,128)}) %all-gather.2.cloned.1.call-update) | async-done | bytes 2097168 | tf_op jit(solution)/shard_map/all_gather | solution.py:22
  62.5 29.2 %all_to_all.5 = f32[4,2,32,2048]{3,2,1,0:T(8,128)S(1)} all-to-all(f32[4,2,32,2048]{3,2,1,0:T(8,128)} %bitcast.17), channel_id=1, replica_groups=mesh['row'=8,'col'=4] {'col'}, dimensions={0} | all-to-all | bytes 4194304 | tf_op jit(solution)/shard_map/all_to_all | solution.py:24
  91.8 0.2 copy.20
  92.0 0.0 copy-done
  92.0 3.6 %convolution_bitcast_fusion = f32[128,2048]{0,1:T(8,128)S(1)} fusion(f32[256,2048]{1,0:T(8,128)S(1)} %bitcast.14, f32[128,256]{1,0:T(8,128)S(1)} %copy-done), kind=kOutput, calls=%fused_computation | convolution fusion | flops 805306368 | bytes 3276800 | tf_op jit(solution)/shard_map/dot_general | solution.py:29
  95.6 1.3 copy.24
  96.9 0.0 reduce-scatter.4.cloned.1.call-update
  96.9 0.0 all-reduce.2.cloned.1.call-start
  97.0 22.5 %reduce-scatter.4.cloned.1.call-done = f32[32,2048]{1,0:T(8,128)} async-done(((f32[128,2048]{1,0:T(8,128)}), f32[32,2048]{1,0:T(8,128)}) %reduce-scatter.4.cloned.1.call-update) | async-done | bytes 262160
  119.5 1.3 copy.25
  120.8 0.1 neg.6
  120.9 0.0 copy-start.1
  120.9 0.3 copy.21
  121.2 0.1 broadcast_multiply_fusion
  121.3 0.0 copy-start.2
  121.4 2.8 %fusion = f32[16,128,128]{2,1,0:T(8,128)} fusion(f32[32,16,128]{2,1,0:T(8,128)S(1)} %broadcast_multiply_fusion, f32[32,16,128]{2,1,0:T(8,128)S(1)} %broadcast_multiply_fusion.1), kind=kOutput, calls=%fused_computation.2 | convolution fusion | flops 100663296 | bytes 1572864 | tf_op jit(solution)/shard_map/bsw,bsv->swv/dot_general | solution.py:38
  124.1 0.0 all-reduce.2.cloned.1.call-update
  124.2 131.8 %all-reduce.2.cloned.1.call-done = f32[16,128,128]{2,1,0:T(8,128)} async-done(((f32[16,128,128]{2,1,0:T(8,128)}), f32[16,128,128]{2,1,0:T(8,128)}) %all-reduce.2.cloned.1.call-update) | async-done | bytes 1048592 | tf_op jit(solution)/shard_map/psum | solution.py:39
  256.0 0.0 copy-done.1
  256.0 2.3 sub.10
  258.3 0.0 copy-done.2
  (2 shorter events, 0.0 us)
Async XLA Ops:
  7.2 84.8 %copy-start = (f32[128,256]{1,0:T(8,128)S(1)}, f32[128,256]{1,0:T(8,128)}, u32[]{:S(2)}) copy-start(f32[128,256]{1,0:T(8,128)} %param.4) | copy-start | bytes 393220
  7.2 55.3 %all-gather.2.cloned.1.call-start = ((), (), s32[]{:S(2)}) async-start(), calls=%async_computation.2 | async-start | bytes 2359296 | tf_op jit(solution)/shard_map/all_gather | solution.py:22
  10.6 108.9 %reduce-scatter.4.cloned.1.call-start = ((), (), s32[]{:S(2)}) async-start(), calls=%async_computation.4 | async-start | bytes 1310720
  96.9 159.1 %all-reduce.2.cloned.1.call-start = ((), (), s32[]{:S(2)}) async-start(), calls=%async_computation.3 | async-start | bytes 2097152 | tf_op jit(solution)/shard_map/psum | solution.py:39
  120.9 135.1 %copy-start.1 = (f32[16,128,128]{2,1,0:T(8,128)S(1)}, f32[16,128,128]{2,1,0:T(8,128)}, u32[]{:S(2)}) copy-start(f32[16,128,128]{2,1,0:T(8,128)} %param.6) | copy-start | bytes 3145732
  121.3 137.0 %copy-start.2 = (f32[32,16,128]{2,1,0:T(8,128)}, f32[32,16,128]{2,1,0:T(8,128)S(1)}, u32[]{:S(2)}) copy-start(f32[32,16,128]{2,1,0:T(8,128)S(1)} %broadcast_multiply_fusion) | copy-start | bytes 786436
Sparse Core Ops, SparseCore 0:
  10.7 51.7 all-gather.1
  97.1 22.3 reduce-scatter.3
  125.3 130.6 all-reduce.1
where the time goes:
time: 265 us
  waiting for transfers between devices  206 us (78%)
  blocking collectives  29.2 us (11%)
  between operations  13.9 us (5%)
  matrix products  6.38 us (2%)
  other arithmetic  4.99 us (2%)
  local copies, waits for them, and re-layouts  3.94 us (1%)
    psum x1, waiting for transfers between devices, per_device(): total_update = lax.psum(local_update, ('row', 'col'))  132 us
    all_gather x1, waiting for transfers between devices, per_device(): strided = lax.all_gather(spread, 'row', axis=0, tiled=True)  51.9 us
    all_to_all x1, blocking collectives, per_device(): lax.all_to_all(grouped, 'col', split_axis=0, concat_axis=0, tiled=True)  29.2 us
    unnamed x4, waiting for transfers between devices  22.6 us
  transfers between devices with their start and end apart: 3, of which 3 were waited for; matrix products, arithmetic and copies ran while one was open for 0% of the time, Pallas kernels for 0%

commit v1 on v0

--- a/solution.py
+++ b/solution.py
@@ -36,7 +36,7 @@
     panel = -summed.reshape(local_rows, count_sib, width)
     panel = panel * row_mask[:, :, None]
     local_update = jnp.einsum("bsw,bsv->swv", masked, panel, precision=lax.Precision.HIGHEST)
-    total_update = lax.psum(local_update, ("row", "col"))
+    total_update = jnp.sum(lax.all_gather(local_update, ("row", "col")), axis=0)
     return (panel, diag_inv - total_update)
 
 

time: 265 us -> 338 us (1.28)
  waiting for transfers between devices: 206 us -> 269 us
  other arithmetic: 4.99 us -> 15.5 us
    all_gather x0 -> x1, waiting for transfers between devices: none -> 194 us  [per_device(): total_update = jnp.sum(lax.all_gather(local_update, ('row', 'col')), axis=0)]
    psum x1 -> x0, waiting for transfers between devices: 132 us -> none  [per_device(): total_update = lax.psum(local_update, ('row', 'col'))]
    reduce_sum x0 -> x1, other arithmetic: none -> 11.7 us  [per_device(): total_update = jnp.sum(lax.all_gather(local_update, ('row', 'col')), axis=0)]
where the time goes in v1:
time: 338 us
  waiting for transfers between devices  269 us (80%)
  blocking collectives  29.2 us (9%)
  other arithmetic  15.5 us (5%)
  between operations  13.9 us (4%)
  matrix products  6.38 us (2%)
  local copies, waits for them, and re-layouts  3.94 us (1%)
    all_gather x1, waiting for transfers between devices, per_device(): total_update = jnp.sum(lax.all_gather(local_update, ('row', 'col')), axis=0)  194 us
    all_gather x1, waiting for transfers between devices, per_device(): strided = lax.all_gather(spread, 'row', axis=0, tiled=True)  51.9 us
    all_to_all x1, blocking collectives, per_device(): lax.all_to_all(grouped, 'col', split_axis=0, concat_axis=0, tiled=True)  29.2 us
    unnamed x4, waiting for transfers between devices  22.6 us
    reduce_sum x1, other arithmetic, per_device(): total_update = jnp.sum(lax.all_gather(local_update, ('row', 'col')), axis=0)  11.7 us
  transfers between devices with their start and end apart: 3, of which 3 were waited for; matrix products, arithmetic and copies ran while one was open for 0% of the time, Pallas kernels for 0%

profile of v1, /device:TPU:0, one launch (start us, length us, event | category | flops | bytes accessed | tf_op | source)
XLA Modules:
  0.0 337.8 jit_solution(2080068341328242271)
XLA Ops:
  7.2 0.0 copy-start
  7.2 0.0 all-gather.4.cloned.1.call-start
  7.2 1.4 compare_reduce_fusion
  8.7 1.1 broadcast_multiply_fusion.1
  9.7 0.8 copy.32
  10.5 0.0 all-gather.4.cloned.1.call-update
  10.6 0.0 reduce-scatter.4.cloned.1.call-start
  10.6 51.9 %all-gather.4.cloned.1.call-done = f32[256,2048]{1,0:T(8,128)} async-done(((f32[32,2048]{1,0:T(8,128)}), f32[256,2048]{1,0:T(8,128)}) %all-gather.4.cloned.1.call-update) | async-done | bytes 2097168 | tf_op jit(solution)/shard_map/all_gather | solution.py:22
  62.5 29.2 %all_to_all.5 = f32[4,2,32,2048]{3,2,1,0:T(8,128)S(1)} all-to-all(f32[4,2,32,2048]{3,2,1,0:T(8,128)} %bitcast.19), channel_id=1, replica_groups=mesh['row'=8,'col'=4] {'col'}, dimensions={0} | all-to-all | bytes 4194304 | tf_op jit(solution)/shard_map/all_to_all | solution.py:24
  91.8 0.2 copy.20
  92.0 0.0 copy-done
  92.0 3.6 %convolution_bitcast_fusion = f32[128,2048]{0,1:T(8,128)S(1)} fusion(f32[256,2048]{1,0:T(8,128)S(1)} %bitcast.16, f32[128,256]{1,0:T(8,128)S(1)} %copy-done), kind=kOutput, calls=%fused_computation | convolution fusion | flops 805306368 | bytes 3276800 | tf_op jit(solution)/shard_map/dot_general | solution.py:29
  95.6 1.3 copy.24
  96.9 0.0 reduce-scatter.4.cloned.1.call-update
  96.9 0.0 all-gather.6.cloned.1.call-start
  97.0 22.5 %reduce-scatter.4.cloned.1.call-done = f32[32,2048]{1,0:T(8,128)} async-done(((f32[128,2048]{1,0:T(8,128)}), f32[32,2048]{1,0:T(8,128)}) %reduce-scatter.4.cloned.1.call-update) | async-done | bytes 262160
  119.5 1.3 copy.25
  120.8 0.1 neg.6
  120.9 0.3 copy.21
  121.2 0.1 broadcast_multiply_fusion
  121.3 0.0 copy-start.2
  121.3 2.8 fusion
  124.1 0.0 all-gather.6.cloned.1.call-update
  124.2 194.3 %all-gather.6.cloned.1.call-done = f32[512,128,128]{2,1,0:T(8,128)} async-done(((f32[16,128,128]{2,1,0:T(8,128)}), f32[512,128,128]{2,1,0:T(8,128)}) %all-gather.6.cloned.1.call-update) | async-done | bytes 33554448 | tf_op jit(solution)/shard_map/all_gather | solution.py:39
  318.5 0.0 copy-start.1
  318.5 11.7 %reduce_sum.9 = f32[16,128,128]{2,1,0:T(8,128)S(1)} reduce(f32[32,16,128,128]{3,2,1,0:T(8,128)} %bitcast.14, f32[]{:T(128)} %constant.32.clone.1), dimensions={0}, to_apply=%region_2.3 | reduce | flops 8126464 | bytes 34603012 | tf_op jit(solution)/shard_map/reduce_sum | solution.py:39
  330.2 0.0 copy-done.2
  330.2 0.0 copy-done.1
  330.2 1.1 sub.10
  (2 shorter events, 0.0 us)
Async XLA Ops:
  7.2 84.8 %copy-start = (f32[128,256]{1,0:T(8,128)S(1)}, f32[128,256]{1,0:T(8,128)}, u32[]{:S(2)}) copy-start(f32[128,256]{1,0:T(8,128)} %param.4) | copy-start | bytes 393220
  7.2 55.3 %all-gather.4.cloned.1.call-start = ((), (), s32[]{:S(2)}) async-start(), calls=%async_computation.2 | async-start | bytes 2359296 | tf_op jit(solution)/shard_map/all_gather | solution.py:22
  10.6 108.9 %reduce-scatter.4.cloned.1.call-start = ((), (), s32[]{:S(2)}) async-start(), calls=%async_computation.4 | async-start | bytes 1310720
  96.9 221.5 %all-gather.6.cloned.1.call-start = ((), (), s32[]{:S(2)}) async-start(), calls=%async_computation.3 | async-start | bytes 34603008 | tf_op jit(solution)/shard_map/all_gather | solution.py:39
  121.3 208.9 %copy-start.2 = (f32[32,16,128]{2,1,0:T(8,128)}, f32[32,16,128]{2,1,0:T(8,128)S(1)}, u32[]{:S(2)}) copy-start(f32[32,16,128]{2,1,0:T(8,128)S(1)} %broadcast_multiply_fusion) | copy-start | bytes 786436
  318.5 11.8 %copy-start.1 = (f32[16,128,128]{2,1,0:T(8,128)S(1)}, f32[16,128,128]{2,1,0:T(8,128)}, u32[]{:S(2)}) copy-start(f32[16,128,128]{2,1,0:T(8,128)} %param.6) | copy-start | bytes 3145732
Sparse Core Ops, SparseCore 0:
  10.7 51.7 all-gather.3
  97.1 22.3 reduce-scatter.3
  124.3 194.1 all-gather.5
